TPU v7x, 32 devices: a whole 2x2x4 slice. The times are simulated.
32 devices in a mesh: groups: 2 (over y), ctx: 16 (over z, x, core).
Axes of the slice: x: 2, y: 2, z: 4, core: 2. Of those that a mesh axis runs over, the one named last changes fastest.
Arguments:
- queries: bfloat16 [16384, 2048], P(('groups', 'ctx')), parts along dimension 0, may hold values from -60 to 60
- keys: bfloat16 [16384, 512], P(('groups', 'ctx')), parts along dimension 0, may hold values from -30 to 30
- values: bfloat16 [16384, 512], P(('groups', 'ctx')), parts along dimension 0, may hold values from -24 to 24
- block_lengths: int32 [32], P(('groups', 'ctx')), parts along dimension 0, may hold values from 256 to 512, as said below
- out_weight: bfloat16 [2048, 4096], P(None, 'ctx'), may hold values from -0.125 to 0.125
Outputs:
- hidden_states: bfloat16 [16384, 4096], P(('groups', 'ctx')), parts along dimension 0
There are 2 independent parts, one for each index of `groups`. A program takes and returns all parts, laid end to end along the dimension named above; an argument that names none is the same for every part. Nothing has to cross between parts.
Inputs may be any that keep to these rules, and one draw needn't show every extreme that they name: `block_lengths`: block 0 always holds 512 valid tokens.
All inputs are finite; a program needn't handle non-finite values.
Results may differ from a plain program's by a relative error of at most 0.0057.
Values may be sent and summed in bfloat16 or wider, within the bound.
A program may use at most 128 MiB of HBM per device.

v0:
```python
import math
import jax
import jax.numpy as jnp
from jax import lax
from jax.sharding import PartitionSpec as P

HD = 128


def broadcast(block, axis, source):
    block = jnp.where(lax.axis_index(axis) == source, block, jnp.zeros_like(block))
    return lax.psum(block, axis)


def make_mask(row_count, valid_length, has_anchor):
    row_ids = jnp.arange(row_count)[:, None]
    col_ids = jnp.arange(row_count)[None, :]
    local_mask = (col_ids <= row_ids) & (col_ids < valid_length)
    anchor_mask = jnp.broadcast_to(has_anchor, (row_count, row_count))
    return jnp.concatenate([anchor_mask, local_mask], axis=1)


def attend(query_rows, key_rows, value_rows, anchor_keys, anchor_values, valid_length, has_anchor):
    row_count = query_rows.shape[0]
    key_heads = key_rows.shape[1] // HD
    group_size = query_rows.shape[1] // key_rows.shape[1]
    query_stack = query_rows.reshape(row_count, key_heads, group_size, HD).transpose(1, 0, 2, 3)
    key_stack = (
        jnp.concatenate([anchor_keys, key_rows], axis=0)
        .reshape(2 * row_count, key_heads, HD)
        .transpose(1, 0, 2)
    )
    value_stack = (
        jnp.concatenate([anchor_values, value_rows], axis=0)
        .reshape(2 * row_count, key_heads, HD)
        .transpose(1, 0, 2)
    )
    visible = make_mask(row_count, valid_length, has_anchor)

    def one_head(operands):
        head_queries, head_keys, head_values = operands
        scores = jnp.einsum(
            "qgd,kd->gqk", head_queries, head_keys, preferred_element_type=jnp.float32
        ) / math.sqrt(HD)
        scores = jnp.where(visible[None], scores, -jnp.inf)
        row_top = jnp.max(scores, axis=-1, keepdims=True)
        exponent = jnp.exp(scores - row_top)
        soft_weights = (exponent / jnp.sum(exponent, axis=-1, keepdims=True)).astype(jnp.bfloat16)
        mixture = jnp.einsum(
            "gqk,kd->qgd", soft_weights, head_values, preferred_element_type=jnp.float32
        )
        return mixture.astype(jnp.bfloat16)

    stacked = lax.map(one_head, (query_stack, key_stack, value_stack))
    return stacked.transpose(1, 0, 2, 3).reshape(row_count, key_heads * group_size * HD)


def per_device(queries, keys, values, block_lengths, out_weight):
    has_anchor = lax.axis_index("ctx") > 0
    anchor_keys, anchor_values = (broadcast(keys, "ctx", 0), broadcast(values, "ctx", 0))
    mixture = attend(
        queries, keys, values, anchor_keys, anchor_values, block_lengths[0], has_anchor
    )
    output = jnp.dot(
        mixture,
        lax.all_gather(out_weight, "ctx", axis=1, tiled=True),
        preferred_element_type=jnp.float32,
    )
    return output.astype(jnp.bfloat16)


def solution(mesh):
    return jax.shard_map(
        per_device,
        mesh=mesh,
        in_specs=(
            P(("groups", "ctx"), None),
            P(("groups", "ctx"), None),
            P(("groups", "ctx"), None),
            P(("groups", "ctx")),
            P(None, "ctx"),
        ),
        out_specs=P(("groups", "ctx"), None),
        check_vma=False,
    )
```

profile of v0, /device:TPU:0, one launch (start us, length us, event | category | flops | bytes accessed | tf_op | source)
XLA Modules:
  0.0 260.0 jit_solution(13996809299489624549)
XLA Ops:
  6.5 0.0 copy-start
  6.5 0.0 all-reduce.4.cloned.1.call-start
  6.5 1.4 copy.11
  7.9 1.3 copy.9
  9.2 1.1 broadcast_select_fusion
  10.3 0.0 all-reduce.4.cloned.1.call-update
  10.3 0.0 all-gather.2.cloned.1.call-start
  10.4 0.7 all-gather.2.cloned.1.call-update
  11.7 0.0 copy-done
  11.7 2.5 copy.13
  14.3 0.1 fusion.39
  14.4 0.9 concatenate.10
  15.3 91.5 %all-reduce.4.cloned.1.call-done = (bf16[512,512]{0,1:T(8,128)(2,1)}, bf16[512,512]{0,1:T(8,128)(2,1)}) async-done(((bf16[512,512]{0,1:T(8,128)(2,1)}, bf16[512,512]{0,1:T(8,128)(2,1)}), (bf16[512,512]{0,1:T(8,128)(2,1)}, bf16[512,512]{0,1:T(8,128)(2,1)})) %all-reduce.4.cloned.1.call-update) | async-done | bytes 1048592 | tf_op jit(solution)/shard_map/psum | solution.py:12
  106.8 1.2 pad_maximum_fusion.1
  108.0 1.2 pad_maximum_fusion
  109.2 50.2 %while.10 = (s32[]{:T(128)}, bf16[4,512,4,128]{1,3,2,0:T(8,128)(2,1)}, bf16[4,1024,128]{1,2,0:T(8,128)(2,1)S(1)}, pred[512,1024]{0,1:T(8,128)(4,1)}, bf16[4,1024...) while((s32[]{:T(128)}, bf16[4,512,4,128]{1,3,2,0:T(8,128)(2,1)}, ...), condition=%wide.region_5.6_spmd, body=%wide.region_2.5_spmd.sunk | while | flops 1086587904 | bytes 18892876 | solution.py:54
  109.2 7.8 %fusion.59 = (f32[4,512]{1,0:T(4,128)S(1)}, f32[4,512,1024]{1,2,0:T(8,128)}) fusion(pred[512,1024]{0,1:T(8,128)(4,1)} %get-tuple-element.120, bf16[4,512,4,128]{1,3,2,0:T(8,128)(2,1)} %get-tuple-element.122, s32[]{:T(128)} %get-tuple-element.110, bf16[4,1024,128]{1,2,0:T(8,128)(2,1)S(1)} %get-tuple-element.121), kind=kOutput, calls=%fused_computation.37.clone.1 | convolution fusion | flops 545260544 | bytes 9708544 | tf_op jit(solution)/shard_map/while/body/eval_jaxpr/sub | solution.py:47
  117.0 5.3 %fusion.60 = bf16[4,512,4,128]{1,3,2,0:T(8,128)(2,1)} fusion(bf16[4,512,4,128]{1,3,2,0:T(8,128)(2,1)} %get-tuple-element.111, s32[]{:T(128)} %get-tuple-element.110, f32[4,512,1024]{1,2,0:T(8,128)} %get-tuple-element.101, f32[4,512]{1,0:T(4,128)S(1)} %get-tuple-element.102, bf16[4,1024,128]{1,2,0:T(8,128)(2,1)S(1)} %get-tuple-element.119), kind=kOutput, calls=%fused_computation.11.clone.1 | convolution fusion | flops 541327360 | bytes 9184256 | tf_op jit(solution)/shard_map/while/body/eval_jaxpr/gqk,kd->qgd/dot_general | solution.py:49
  122.2 7.5 %fusion.59 = (f32[4,512]{1,0:T(4,128)S(1)}, f32[4,512,1024]{1,2,0:T(8,128)}) fusion(pred[512,1024]{0,1:T(8,128)(4,1)} %get-tuple-element.120, bf16[4,512,4,128]{1,3,2,0:T(8,128)(2,1)} %get-tuple-element.122, s32[]{:T(128)} %get-tuple-element.110, bf16[4,1024,128]{1,2,0:T(8,128)(2,1)S(1)} %get-tuple-element.121), kind=kOutput, calls=%fused_computation.37.clone.1 | convolution fusion | flops 545260544 | bytes 9708544 | tf_op jit(solution)/shard_map/while/body/eval_jaxpr/sub | solution.py:47
  129.7 5.0 %fusion.60 = bf16[4,512,4,128]{1,3,2,0:T(8,128)(2,1)} fusion(bf16[4,512,4,128]{1,3,2,0:T(8,128)(2,1)} %get-tuple-element.111, s32[]{:T(128)} %get-tuple-element.110, f32[4,512,1024]{1,2,0:T(8,128)} %get-tuple-element.101, f32[4,512]{1,0:T(4,128)S(1)} %get-tuple-element.102, bf16[4,1024,128]{1,2,0:T(8,128)(2,1)S(1)} %get-tuple-element.119), kind=kOutput, calls=%fused_computation.11.clone.1 | convolution fusion | flops 541327360 | bytes 9184256 | tf_op jit(solution)/shard_map/while/body/eval_jaxpr/gqk,kd->qgd/dot_general | solution.py:49
  134.7 7.5 %fusion.59 = (f32[4,512]{1,0:T(4,128)S(1)}, f32[4,512,1024]{1,2,0:T(8,128)}) fusion(pred[512,1024]{0,1:T(8,128)(4,1)} %get-tuple-element.120, bf16[4,512,4,128]{1,3,2,0:T(8,128)(2,1)} %get-tuple-element.122, s32[]{:T(128)} %get-tuple-element.110, bf16[4,1024,128]{1,2,0:T(8,128)(2,1)S(1)} %get-tuple-element.121), kind=kOutput, calls=%fused_computation.37.clone.1 | convolution fusion | flops 545260544 | bytes 9708544 | tf_op jit(solution)/shard_map/while/body/eval_jaxpr/sub | solution.py:47
  142.2 4.9 %fusion.60 = bf16[4,512,4,128]{1,3,2,0:T(8,128)(2,1)} fusion(bf16[4,512,4,128]{1,3,2,0:T(8,128)(2,1)} %get-tuple-element.111, s32[]{:T(128)} %get-tuple-element.110, f32[4,512,1024]{1,2,0:T(8,128)} %get-tuple-element.101, f32[4,512]{1,0:T(4,128)S(1)} %get-tuple-element.102, bf16[4,1024,128]{1,2,0:T(8,128)(2,1)S(1)} %get-tuple-element.119), kind=kOutput, calls=%fused_computation.11.clone.1 | convolution fusion | flops 541327360 | bytes 9184256 | tf_op jit(solution)/shard_map/while/body/eval_jaxpr/gqk,kd->qgd/dot_general | solution.py:49
  147.1 7.5 %fusion.59 = (f32[4,512]{1,0:T(4,128)S(1)}, f32[4,512,1024]{1,2,0:T(8,128)}) fusion(pred[512,1024]{0,1:T(8,128)(4,1)} %get-tuple-element.120, bf16[4,512,4,128]{1,3,2,0:T(8,128)(2,1)} %get-tuple-element.122, s32[]{:T(128)} %get-tuple-element.110, bf16[4,1024,128]{1,2,0:T(8,128)(2,1)S(1)} %get-tuple-element.121), kind=kOutput, calls=%fused_computation.37.clone.1 | convolution fusion | flops 545260544 | bytes 9708544 | tf_op jit(solution)/shard_map/while/body/eval_jaxpr/sub | solution.py:47
  154.6 4.9 %fusion.60 = bf16[4,512,4,128]{1,3,2,0:T(8,128)(2,1)} fusion(bf16[4,512,4,128]{1,3,2,0:T(8,128)(2,1)} %get-tuple-element.111, s32[]{:T(128)} %get-tuple-element.110, f32[4,512,1024]{1,2,0:T(8,128)} %get-tuple-element.101, f32[4,512]{1,0:T(4,128)S(1)} %get-tuple-element.102, bf16[4,1024,128]{1,2,0:T(8,128)(2,1)S(1)} %get-tuple-element.119), kind=kOutput, calls=%fused_computation.11.clone.1 | convolution fusion | flops 541327360 | bytes 9184256 | tf_op jit(solution)/shard_map/while/body/eval_jaxpr/gqk,kd->qgd/dot_general | solution.py:49
  159.4 79.2 %all-gather.2.cloned.1.call-done = bf16[2048,4096]{1,0:T(8,128)(2,1)} async-done(((bf16[2048,256]{1,0:T(8,128)(2,1)}), bf16[2048,4096]{1,0:T(8,128)(2,1)}) %all-gather.2.cloned.1.call-update) | async-done | bytes 16777232 | tf_op jit(solution)/shard_map/all_gather | solution.py:66
  238.7 14.5 %convolution_convert_fusion = bf16[512,4096]{1,0:T(8,128)(2,1)} fusion(bf16[512,2048]{0,1:T(8,128)(2,1)} %bitcast.77, bf16[2048,4096]{1,0:T(8,128)(2,1)} %all-gather.2.cloned.1.call-done), kind=kOutput, calls=%fused_computation.29 | convolution fusion | flops 8592031744 | bytes 23068672 | tf_op jit(solution)/shard_map/dot_general | solution.py:64
  (2 shorter events, 0.0 us)
Async XLA Ops:
  6.5 5.2 %copy-start = (bf16[512,2048]{1,0:T(8,128)(2,1)S(1)}, bf16[512,2048]{1,0:T(8,128)(2,1)}, u32[]{:S(2)}) copy-start(bf16[512,2048]{1,0:T(8,128)(2,1)} %param.7) | copy-start | bytes 6291460
  6.5 100.3 %all-reduce.4.cloned.1.call-start = ((), (), s32[]{:S(2)}) async-start(), calls=%async_computation.1 | async-start | bytes 2097152 | tf_op jit(solution)/shard_map/psum | solution.py:12
  10.3 228.3 %all-gather.2.cloned.1.call-start = ((), (), s32[]{:S(2)}) async-start(), calls=%async_computation | async-start | bytes 17825792 | tf_op jit(solution)/shard_map/all_gather | solution.py:66
Sparse Core Ops, SparseCore 0:
  10.9 95.8 all-reduce.3
  109.0 129.6 all-gather.1
where the time goes:
time: 260 us
  waiting for transfers between devices  171 us (66%)
  matrix products  64.7 us (25%)
  between operations  14.1 us (5%)
  local copies, waits for them, and re-layouts  6.06 us (2%)
  other arithmetic  3.6 us (1%)
    psum x1, waiting for transfers between devices, broadcast(): return lax.psum(block, axis)  91.5 us
    all_gather x1, waiting for transfers between devices, per_device(): lax.all_gather(out_weight, 'ctx', axis=1, tiled=True)  79.2 us
    sub x4, matrix products, one_head(): exponent = jnp.exp(scores - row_top)  30.2 us
    dot_general x4, matrix products, one_head(): jnp.einsum('gqk,kd->qgd', soft_weights, head_values, preferred_element_ty...  20.1 us
    dot_general x1, matrix products, per_device(): jnp.dot(mixture, lax.all_gather(out_weight, 'ctx', axis=1, tiled=True), p...  14.5 us
  transfers between devices with their start and end apart: 2, of which 2 were waited for; matrix products, arithmetic and copies ran while one was open for 22% of the time, Pallas kernels for 0%

commit v1 on v0

--- a/solution.py
+++ b/solution.py
@@ -9,7 +9,10 @@
 
 def broadcast(block, axis, source):
     block = jnp.where(lax.axis_index(axis) == source, block, jnp.zeros_like(block))
-    return lax.psum(block, axis)
+    define_the_record = lambda content, peer_axis: lax.all_gather(content, axis_name=peer_axis).sum(
+        axis=0
+    )
+    return define_the_record(block, peer_axis=axis)
 
 
 def make_mask(row_count, valid_length, has_anchor):

time: 260 us -> 315 us (1.21)
  waiting for transfers between devices: 171 us -> 217 us
  other arithmetic: 3.6 us -> 13.9 us
    all_gather x0 -> x2, waiting for transfers between devices: none -> 141 us  [broadcast(): lax.all_gather(content, axis_name=peer_axis).sum(axis=0)]
    psum x1 -> x0, waiting for transfers between devices: 91.5 us -> none  [broadcast(): return lax.psum(block, axis)]
    reduce_sum x0 -> x2, other arithmetic: none -> 9.76 us  [broadcast(): lax.all_gather(content, axis_name=peer_axis).sum(axis=0)]
    all_gather x1, waiting for transfers between devices: 79.2 us -> 74.6 us  [per_device(): lax.all_gather(out_weight, 'ctx', axis=1, tiled=True)]
  transfers between devices with their start and end apart: 2 -> 3, of which waited for: 2 -> 3; matrix products, arithmetic and copies ran while one was open for 22% -> 21% of each run, Pallas kernels for 0% -> 0%
where the time goes in v1:
time: 315 us; the launch traced here: 314 us
  waiting for transfers between devices  217 us (69%)
  matrix products  65.1 us (21%)
  other arithmetic  13.9 us (4%)
  between operations  13.8 us (4%)
  local copies, waits for them, and re-layouts  4.49 us (1%)
    all_gather x2, waiting for transfers between devices, broadcast(): lax.all_gather(content, axis_name=peer_axis).sum(axis=0)  141 us
    all_gather x1, waiting for transfers between devices, per_device(): lax.all_gather(out_weight, 'ctx', axis=1, tiled=True)  74.6 us
    sub x4, matrix products, one_head(): exponent = jnp.exp(scores - row_top)  29.9 us
    dot_general x4, matrix products, one_head(): jnp.einsum('gqk,kd->qgd', soft_weights, head_values, preferred_element_ty...  20.8 us
    dot_general x1, matrix products, per_device(): jnp.dot(mixture, lax.all_gather(out_weight, 'ctx', axis=1, tiled=True), p...  14.5 us
    reduce_sum x2, other arithmetic, broadcast(): lax.all_gather(content, axis_name=peer_axis).sum(axis=0)  9.76 us
  transfers between devices with their start and end apart: 3, of which 3 were waited for; matrix products, arithmetic and copies ran while one was open for 21% of the time, Pallas kernels for 0%

profile of v1, /device:TPU:0, one launch (start us, length us, event | category | flops | bytes accessed | tf_op | source)
XLA Modules:
  0.0 314.3 jit_solution(5116936803249667406)
XLA Ops:
  6.5 0.0 all-gather.8.cloned.1.call-start
  6.5 2.0 broadcast_select_fusion.1
  8.6 0.0 all-gather.8.cloned.1.call-update
  8.6 0.0 all-gather.10.cloned.1.call-start
  8.6 1.9 broadcast_select_fusion
  10.5 0.0 all-gather.10.cloned.1.call-update
  10.5 0.0 all-gather.6.cloned.1.call-start
  10.6 0.7 all-gather.6.cloned.1.call-update
  11.9 0.0 copy-done
  11.9 2.5 copy.17
  14.4 0.1 fusion.39
  14.6 0.9 concatenate.10
  15.5 71.7 %all-gather.8.cloned.1.call-done = bf16[8192,512]{1,0:T(8,128)(2,1)} async-done(((bf16[512,512]{1,0:T(8,128)(2,1)}), bf16[8192,512]{1,0:T(8,128)(2,1)}) %all-gather.8.cloned.1.call-update) | async-done | bytes 8388624 | tf_op jit(solution)/shard_map/all_gather | solution.py:12
  87.1 4.9 %reduce_sum.33 = bf16[512,512]{1,0:T(8,128)(2,1)S(1)} reduce(bf16[16,512,512]{2,1,0:T(8,128)(2,1)} %bitcast.76, bf16[]{:T(256)} %constant.29.clone.1), dimensions={0}, to_apply=%region_1.2 | reduce | flops 3932160 | bytes 8912898 | tf_op jit(solution)/shard_map/reduce_sum | solution.py:12
  92.0 0.0 copy-done.1
  92.0 0.1 pad_maximum_fusion
  92.1 0.5 copy.15
  92.7 69.8 %all-gather.10.cloned.1.call-done = bf16[8192,512]{1,0:T(8,128)(2,1)} async-done(((bf16[512,512]{1,0:T(8,128)(2,1)}), bf16[8192,512]{1,0:T(8,128)(2,1)}) %all-gather.10.cloned.1.call-update) | async-done | bytes 8388624 | tf_op jit(solution)/shard_map/all_gather | solution.py:12
  162.5 4.9 %reduce_sum.34 = bf16[512,512]{1,0:T(8,128)(2,1)S(1)} reduce(bf16[16,512,512]{2,1,0:T(8,128)(2,1)} %bitcast.77, bf16[]{:T(256)} %constant.29.clone.1), dimensions={0}, to_apply=%region_0.1 | reduce | flops 3932160 | bytes 8912898 | tf_op jit(solution)/shard_map/reduce_sum | solution.py:12
  167.4 0.1 pad_maximum_fusion.1
  167.5 0.5 copy.16
  168.0 50.7 %while.10 = (s32[]{:T(128)}, bf16[4,512,4,128]{1,3,2,0:T(8,128)(2,1)}, bf16[4,1024,128]{1,2,0:T(8,128)(2,1)S(1)}, pred[512,1024]{0,1:T(8,128)(4,1)}, bf16[4,1024...) while((s32[]{:T(128)}, bf16[4,512,4,128]{1,3,2,0:T(8,128)(2,1)}, ...), condition=%wide.region_5.6_spmd, body=%wide.region_2.5_spmd.sunk | while | flops 1086587904 | bytes 18892876 | solution.py:57
  168.0 7.5 %fusion.59 = (f32[4,512]{1,0:T(4,128)S(1)}, f32[4,512,1024]{1,2,0:T(8,128)}) fusion(pred[512,1024]{0,1:T(8,128)(4,1)} %get-tuple-element.122, bf16[4,512,4,128]{1,3,2,0:T(8,128)(2,1)} %get-tuple-element.124, s32[]{:T(128)} %get-tuple-element.112, bf16[4,1024,128]{1,2,0:T(8,128)(2,1)S(1)} %get-tuple-element.123), kind=kOutput, calls=%fused_computation.37.clone.1 | convolution fusion | flops 545260544 | bytes 9708544 | tf_op jit(solution)/shard_map/while/body/eval_jaxpr/sub | solution.py:50
  175.5 4.9 %fusion.60 = bf16[4,512,4,128]{1,3,2,0:T(8,128)(2,1)} fusion(bf16[4,512,4,128]{1,3,2,0:T(8,128)(2,1)} %get-tuple-element.113, s32[]{:T(128)} %get-tuple-element.112, f32[4,512,1024]{1,2,0:T(8,128)} %get-tuple-element.103, f32[4,512]{1,0:T(4,128)S(1)} %get-tuple-element.104, bf16[4,1024,128]{1,2,0:T(8,128)(2,1)S(1)} %get-tuple-element.121), kind=kOutput, calls=%fused_computation.11.clone.1 | convolution fusion | flops 541327360 | bytes 9184256 | tf_op jit(solution)/shard_map/while/body/eval_jaxpr/gqk,kd->qgd/dot_general | solution.py:52
  180.4 7.5 %fusion.59 = (f32[4,512]{1,0:T(4,128)S(1)}, f32[4,512,1024]{1,2,0:T(8,128)}) fusion(pred[512,1024]{0,1:T(8,128)(4,1)} %get-tuple-element.122, bf16[4,512,4,128]{1,3,2,0:T(8,128)(2,1)} %get-tuple-element.124, s32[]{:T(128)} %get-tuple-element.112, bf16[4,1024,128]{1,2,0:T(8,128)(2,1)S(1)} %get-tuple-element.123), kind=kOutput, calls=%fused_computation.37.clone.1 | convolution fusion | flops 545260544 | bytes 9708544 | tf_op jit(solution)/shard_map/while/body/eval_jaxpr/sub | solution.py:50
  187.9 5.0 %fusion.60 = bf16[4,512,4,128]{1,3,2,0:T(8,128)(2,1)} fusion(bf16[4,512,4,128]{1,3,2,0:T(8,128)(2,1)} %get-tuple-element.113, s32[]{:T(128)} %get-tuple-element.112, f32[4,512,1024]{1,2,0:T(8,128)} %get-tuple-element.103, f32[4,512]{1,0:T(4,128)S(1)} %get-tuple-element.104, bf16[4,1024,128]{1,2,0:T(8,128)(2,1)S(1)} %get-tuple-element.121), kind=kOutput, calls=%fused_computation.11.clone.1 | convolution fusion | flops 541327360 | bytes 9184256 | tf_op jit(solution)/shard_map/while/body/eval_jaxpr/gqk,kd->qgd/dot_general | solution.py:52
  192.9 7.5 %fusion.59 = (f32[4,512]{1,0:T(4,128)S(1)}, f32[4,512,1024]{1,2,0:T(8,128)}) fusion(pred[512,1024]{0,1:T(8,128)(4,1)} %get-tuple-element.122, bf16[4,512,4,128]{1,3,2,0:T(8,128)(2,1)} %get-tuple-element.124, s32[]{:T(128)} %get-tuple-element.112, bf16[4,1024,128]{1,2,0:T(8,128)(2,1)S(1)} %get-tuple-element.123), kind=kOutput, calls=%fused_computation.37.clone.1 | convolution fusion | flops 545260544 | bytes 9708544 | tf_op jit(solution)/shard_map/while/body/eval_jaxpr/sub | solution.py:50
  200.3 5.0 %fusion.60 = bf16[4,512,4,128]{1,3,2,0:T(8,128)(2,1)} fusion(bf16[4,512,4,128]{1,3,2,0:T(8,128)(2,1)} %get-tuple-element.113, s32[]{:T(128)} %get-tuple-element.112, f32[4,512,1024]{1,2,0:T(8,128)} %get-tuple-element.103, f32[4,512]{1,0:T(4,128)S(1)} %get-tuple-element.104, bf16[4,1024,128]{1,2,0:T(8,128)(2,1)S(1)} %get-tuple-element.121), kind=kOutput, calls=%fused_computation.11.clone.1 | convolution fusion | flops 541327360 | bytes 9184256 | tf_op jit(solution)/shard_map/while/body/eval_jaxpr/gqk,kd->qgd/dot_general | solution.py:52
  205.3 7.5 %fusion.59 = (f32[4,512]{1,0:T(4,128)S(1)}, f32[4,512,1024]{1,2,0:T(8,128)}) fusion(pred[512,1024]{0,1:T(8,128)(4,1)} %get-tuple-element.122, bf16[4,512,4,128]{1,3,2,0:T(8,128)(2,1)} %get-tuple-element.124, s32[]{:T(128)} %get-tuple-element.112, bf16[4,1024,128]{1,2,0:T(8,128)(2,1)S(1)} %get-tuple-element.123), kind=kOutput, calls=%fused_computation.37.clone.1 | convolution fusion | flops 545260544 | bytes 9708544 | tf_op jit(solution)/shard_map/while/body/eval_jaxpr/sub | solution.py:50
  212.8 5.9 %fusion.60 = bf16[4,512,4,128]{1,3,2,0:T(8,128)(2,1)} fusion(bf16[4,512,4,128]{1,3,2,0:T(8,128)(2,1)} %get-tuple-element.113, s32[]{:T(128)} %get-tuple-element.112, f32[4,512,1024]{1,2,0:T(8,128)} %get-tuple-element.103, f32[4,512]{1,0:T(4,128)S(1)} %get-tuple-element.104, bf16[4,1024,128]{1,2,0:T(8,128)(2,1)S(1)} %get-tuple-element.121), kind=kOutput, calls=%fused_computation.11.clone.1 | convolution fusion | flops 541327360 | bytes 9184256 | tf_op jit(solution)/shard_map/while/body/eval_jaxpr/gqk,kd->qgd/dot_general | solution.py:52
  218.7 74.6 %all-gather.6.cloned.1.call-done = bf16[2048,4096]{1,0:T(8,128)(2,1)} async-done(((bf16[2048,256]{1,0:T(8,128)(2,1)}), bf16[2048,4096]{1,0:T(8,128)(2,1)}) %all-gather.6.cloned.1.call-update) | async-done | bytes 16777232 | tf_op jit(solution)/shard_map/all_gather | solution.py:69
  293.3 14.5 %convolution_convert_fusion = bf16[512,4096]{1,0:T(8,128)(2,1)} fusion(bf16[512,2048]{0,1:T(8,128)(2,1)} %bitcast.81, bf16[2048,4096]{1,0:T(8,128)(2,1)} %all-gather.6.cloned.1.call-done), kind=kOutput, calls=%fused_computation.29 | convolution fusion | flops 8592031744 | bytes 23068672 | tf_op jit(solution)/shard_map/dot_general | solution.py:67
  (6 shorter events, 0.0 us)
Async XLA Ops:
  6.5 5.4 %copy-start = (bf16[512,2048]{1,0:T(8,128)(2,1)S(1)}, bf16[512,2048]{1,0:T(8,128)(2,1)}, u32[]{:S(2)}) copy-start(bf16[512,2048]{1,0:T(8,128)(2,1)} %param.7) | copy-start | bytes 6291460
  6.5 80.6 %all-gather.8.cloned.1.call-start = ((), (), s32[]{:S(2)}) async-start(), calls=%async_computation.1 | async-start | bytes 8912896 | tf_op jit(solution)/shard_map/all_gather | solution.py:12
  8.6 153.9 %all-gather.10.cloned.1.call-start = ((), (), s32[]{:S(2)}) async-start(), calls=%async_computation.2 | async-start | bytes 8912896 | tf_op jit(solution)/shard_map/all_gather | solution.py:12
  10.5 282.7 %all-gather.6.cloned.1.call-start = ((), (), s32[]{:S(2)}) async-start(), calls=%async_computation | async-start | bytes 17825792 | tf_op jit(solution)/shard_map/all_gather | solution.py:69
  87.1 4.9 %copy-start.1 = (bf16[512,512]{1,0:T(8,128)(2,1)S(1)}, bf16[512,512]{1,0:T(8,128)(2,1)}, u32[]{:S(2)}) copy-start(bf16[512,512]{1,0:T(8,128)(2,1)} %param.9) | copy-start | bytes 1572868
  162.5 4.9 %copy-start.2 = (bf16[512,512]{1,0:T(8,128)(2,1)S(1)}, bf16[512,512]{1,0:T(8,128)(2,1)}, u32[]{:S(2)}) copy-start(bf16[512,512]{1,0:T(8,128)(2,1)} %param.8) | copy-start | bytes 1572868
Sparse Core Ops, SparseCore 0:
  9.5 77.5 all-gather.7
  89.3 73.1 all-gather.9
  164.6 128.5 all-gather.5
